TPU v7x, 128 devices: a whole 4x4x4 slice. The times are simulated.
128 devices in a mesh: grp: 16 (over x, y), chan: 8 (over z, core).
Axes of the slice: x: 4, y: 4, z: 4, core: 2. Of those that a mesh axis runs over, the one named last changes fastest.
Arguments:
- spectra: bfloat16 [2048, 2, 2, 8192], P(('grp', 'chan')), may hold values from -45 to 45
- pair_blocks: int32 [16, 8, 18, 2], P('grp', 'chan'), may hold values from 0 to 63
- owners: int32 [16, 8, 18, 1], P('grp', 'chan'), may hold values from 0 to 15; in each aligned block of 18 rows (0 to 17, 18 to 35, ..., all dimensions but the last counted through in order) at most 3 rows name the same one
Outputs:
- stacks: float32 [16, 8, 48, 4, 1024], P('grp', 'chan')
Inputs may be any that keep to these rules, and one draw needn't show every extreme that they name: `owners`: at most 3 of one device's 18 pair blocks name the same owner.
All inputs are finite; a program needn't handle non-finite values.
Results may differ from a plain program's by a relative error of at most 0.011.
Values may be sent and summed in bfloat16 or wider, within the bound.
A program may use at most 128 MiB of HBM per device.

v0:
```python
import jax
import jax.numpy as jnp
from jax import lax
from jax.sharding import PartitionSpec as P

F = 8192
LAGS = 1024
BLK = 2
NB_SRC = 18
MOST = 3
WINDOWS = 2


def table_block(start, count):
    bins = start + jnp.arange(count, dtype=jnp.int32)
    lag_index = jnp.arange(LAGS, dtype=jnp.int32) - LAGS // 2
    phase = bins[:, None] * lag_index[None, :] % (2 * F)
    angle = phase.astype(jnp.float32) * (jnp.pi / F)
    weight = jnp.where(bins == 0, 1.0, 2.0).astype(jnp.float32) / jnp.sqrt(jnp.float32(F))
    cos_part = (jnp.cos(angle) * weight[:, None]).astype(jnp.bfloat16)
    sin_part = (-jnp.sin(angle) * weight[:, None]).astype(jnp.bfloat16)
    return (cos_part, sin_part)


def to_lags(rows):
    width_block = min(512, F)
    real_rows = rows[:, 0]
    imag_rows = rows[:, 1]

    def add_block(turn, total):
        start = (turn * width_block).astype(jnp.int32)
        cos_part, sin_part = table_block(start, width_block)
        real_slice = lax.dynamic_slice_in_dim(real_rows, start, width_block, 1)
        imag_slice = lax.dynamic_slice_in_dim(imag_rows, start, width_block, 1)
        total = total + jnp.dot(real_slice, cos_part, preferred_element_type=jnp.float32)
        return total + jnp.dot(imag_slice, sin_part, preferred_element_type=jnp.float32)

    start_total = jnp.zeros((rows.shape[0], LAGS), jnp.float32)
    return lax.fori_loop(0, F // width_block, add_block, start_total)


def whiten(spectra):
    values = spectra.astype(jnp.float32)
    power = values[:, :, 0] ** 2 + values[:, :, 1] ** 2
    level = jnp.mean(power, axis=-1, keepdims=True) + 1e-05
    scale = lax.rsqrt(power + 0.1 * level)
    return (values * scale[:, :, None, :]).astype(jnp.bfloat16)


def cross_pairs(left, right):
    real_left = left[..., :, None, :, 0, :]
    imag_left = left[..., :, None, :, 1, :]
    real_right = right[..., None, :, :, 0, :]
    imag_right = right[..., None, :, :, 1, :]
    real_part = real_left * real_right + imag_left * imag_right
    imag_part = imag_left * real_right - real_left * imag_right
    both = jnp.stack([real_part, imag_part], axis=-2)
    return both.astype(jnp.bfloat16)


def local(spectra, pair_blocks, owners):
    groups_count = lax.axis_size("grp")
    slot_count = groups_count * MOST
    white = whiten(spectra)
    panel = lax.all_gather(white, "chan", axis=0, tiled=True)
    blocks = pair_blocks[0, 0]
    offsets = jnp.arange(BLK, dtype=jnp.int32)
    left_idx = blocks[:, 0][:, None] * BLK + offsets
    right_idx = blocks[:, 1][:, None] * BLK + offsets
    left = jnp.take(panel, left_idx, axis=0).astype(jnp.float32)
    right = jnp.take(panel, right_idx, axis=0).astype(jnp.float32)
    cross = cross_pairs(left, right).reshape(NB_SRC, BLK * BLK, WINDOWS, 2, F)
    owner_list = owners[0, 0, :, 0]
    same = owner_list[:, None] == owner_list[None, :]
    earlier = jnp.arange(NB_SRC)[None, :] < jnp.arange(NB_SRC)[:, None]
    order_rank = jnp.sum(jnp.logical_and(same, earlier), axis=1)
    slot_ids = owner_list * MOST + order_rank
    chooser = slot_ids[None, :] == jnp.arange(slot_count, dtype=jnp.int32)[:, None]
    pairs = BLK * BLK
    summed = jnp.zeros((groups_count, MOST, pairs, 2, F), jnp.float32)
    for window in range(WINDOWS):
        placed = jnp.einsum(
            "ms,sprf->mprf",
            chooser.astype(jnp.bfloat16),
            cross[:, :, window],
            preferred_element_type=jnp.float32,
        )
        summed = summed + lax.all_to_all(
            placed.astype(jnp.bfloat16).reshape(groups_count, MOST, pairs, 2, F),
            "grp",
            split_axis=0,
            concat_axis=0,
            tiled=True,
        ).astype(jnp.float32)
    received = (summed / WINDOWS).astype(jnp.bfloat16)
    shape_now = received.shape
    rows = received.reshape(-1, 2, F)
    result = to_lags(rows).reshape(shape_now[0], shape_now[1], pairs, LAGS)
    return result.reshape(1, 1, slot_count, pairs, LAGS)


def solution(mesh):
    return jax.shard_map(
        local,
        mesh=mesh,
        in_specs=(
            P(("grp", "chan"), None, None, None),
            P("grp", "chan", None, None),
            P("grp", "chan", None, None),
        ),
        out_specs=P("grp", "chan", None, None, None),
        check_vma=False,
    )
```

profile of v0, /device:TPU:20, one launch (start us, length us, event | category | flops | bytes accessed | tf_op | source)
XLA Modules:
  0.0 685.6 jit_solution(13492980502422854776)
XLA Ops:
  13.3 51.4 %all-gather.2.cloned.1.call-done = bf16[128,2,2,8192]{3,2,1,0:T(2,128)(2,1)} async-done(((bf16[16,2,2,8192]{3,2,1,0:T(2,128)(2,1)}), bf16[128,2,2,8192]{3,2,1,0:T(2,128)(2,1)}) %all-gather.2.cloned.1.call-update) | async-done | bytes 8388624 | tf_op jit(solution)/shard_map/all_gather | solution.py:65
  64.7 11.3 %gather_fusion = bf16[36,2,2,8192]{3,2,1,0:T(2,128)(2,1)S(1)} fusion(bf16[128,2,2,8192]{3,2,1,0:T(2,128)(2,1)} %all-gather.2.cloned.1.call-done, s32[1024]{0:T(1024)S(1)} %pad_clamp_fusion.1), kind=kCustom, calls=%fused_computation.clone | custom fusion | bytes 4718736 | tf_op jit(solution)/shard_map/jit(_take)/gather | solution.py:70
  90.0 11.5 %gather_fusion.1 = bf16[36,2,2,8192]{3,2,1,0:T(2,128)(2,1)S(1)} fusion(bf16[128,2,2,8192]{3,2,1,0:T(2,128)(2,1)} %all-gather.2.cloned.1.call-done, s32[1024]{0:T(1024)S(1)} %pad_clamp_fusion), kind=kCustom, calls=%fused_computation.1.clone | custom fusion | bytes 4718736 | tf_op jit(solution)/shard_map/jit(_take)/gather | solution.py:71
  116.5 11.0 %copy.58 = bf16[48,4,2,8192]{3,2,1,0:T(2,128)(2,1)} copy(bf16[48,4,2,8192]{3,0,2,1:T(8,128)(2,1)S(1)} %convolution_convert_fusion.1) | data formatting | bytes 12582912 | tf_op jit(solution)/shard_map/convert_element_type | solution.py:89
  138.0 11.0 %copy.59 = bf16[48,4,2,8192]{3,2,1,0:T(2,128)(2,1)} copy(bf16[48,4,2,8192]{3,0,2,1:T(8,128)(2,1)S(1)} %convolution_convert_fusion) | data formatting | bytes 12582912 | tf_op jit(solution)/shard_map/convert_element_type | solution.py:89
  149.0 89.4 %all-to-all-done = bf16[16,3,4,2,8192]{4,3,2,1,0:T(2,128)(2,1)} async-done(((bf16[16,3,4,2,8192]{4,3,2,1,0:T(2,128)(2,1)}), bf16[16,3,4,2,8192]{4,3,2,1,0:T(2,128)(2,1)}, u32[]{:S(2)}, u32[]{:S(2)}) %all-to-all-start) | async-done | bytes 6291488 | tf_op jit(solution)/shard_map/all_to_all | solution.py:88
  238.5 14.3 %all-to-all-start.1 = ((bf16[16,3,4,2,8192]{4,3,2,1,0:T(2,128)(2,1)}), bf16[16,3,4,2,8192]{4,3,2,1,0:T(2,128)(2,1)}, u32[]{:S(2)}, u32[]{:S(2)}) async-start(bf16[16,3,4,2,8192]{4,3,2,1,0:T(2,128)(2,1)} %bitcast.51), calls=%async_computation.1 | async-start | bytes 12582912 | tf_op jit(solution)/shard_map/all_to_all | solution.py:88
  252.8 99.9 %all-to-all-done.1 = bf16[16,3,4,2,8192]{4,3,2,1,0:T(2,128)(2,1)} async-done(((bf16[16,3,4,2,8192]{4,3,2,1,0:T(2,128)(2,1)}), bf16[16,3,4,2,8192]{4,3,2,1,0:T(2,128)(2,1)}, u32[]{:S(2)}, u32[]{:S(2)}) %all-to-all-start.1) | async-done | bytes 6291488 | tf_op jit(solution)/shard_map/all_to_all | solution.py:88
  352.7 11.2 %multiply_convert_fusion.4 = bf16[16,3,4,2,8192]{4,3,2,1,0:T(2,128)(2,1)S(1)} fusion(bf16[16,3,4,2,8192]{4,3,2,1,0:T(2,128)(2,1)} %all-to-all-done.1, bf16[16,3,4,2,8192]{4,3,2,1,0:T(2,128)(2,1)} %all-to-all-done), kind=kLoop, calls=%fused_computation.29 | loop fusion | flops 15728640 | bytes 18874368 | tf_op jit(solution)/shard_map/convert_element_type | solution.py:95
  363.9 13.4 %fusion.35 = (bf16[192,1,8192]{2,1,0:T(2,128)(2,1)S(1)}, bf16[192,1,8192]{2,1,0:T(2,128)(2,1)S(1)}) fusion(bf16[192,2,8192]{2,1,0:T(2,128)(2,1)S(1)} %bitcast.46), kind=kLoop, calls=%fused_computation.77 | loop fusion | bytes 12582912 | tf_op jit(solution)/shard_map/slice | solution.py:28
  385.9 290.4 %while.16 = (s32[]{:T(128)}, f32[192,1024]{1,0:T(8,128)}, bf16[192,8192]{1,0:T(8,128)(2,1)}, bf16[192,8192]{1,0:T(8,128)(2,1)S(1)}, s32[]{:T(128)}, /*index=5*/s32[]{:T(128)}, s32[]{:T(128)}, s32[]{:T(128)}) while((s32[]{:T(128)}, f32[192,1024]{1,0:T(8,128)}, bf16[192,8192]{1,0:T(8,128)(2,1)}, bf16[192,8192]{1,0:T(8,128)(2,1)S(1)}, ...), condition=%wide.region_3.5_spmd.clone, body=%wide.region_2.4_spmd.clone.sunk | while | flops 420548096 | bytes 3563677 | solution.py:39
  395.0 9.0 %convolution_add_fusion.5 = f32[192,1024]{1,0:T(8,128)} fusion(f32[192,1024]{1,0:T(8,128)S(1)} %convolution_add_fusion.4, f32[512]{0:T(512)S(1)} %select_multiply_fusion.2, s32[1024]{0:T(1024)S(1)} %iota_add_fusion.4, s32[512]{0:T(512)S(1)} %iota_add_fusion.5, bf16[192,8192]{1,0:T(8,128)(2,1)S(1)} %get-tuple-element.200, s32[]{:T(128)S(6)} %select_n.93), kind=kOutput, calls=%fused_computation.12.clone.1 | convolution fusion | flops 210436096 | bytes 1777668 | tf_op jit(solution)/shard_map/while/body/eval_jaxpr/dot_general | solution.py:36
  403.9 9.2 %convolution_add_fusion.4 = f32[192,1024]{1,0:T(8,128)S(1)} fusion(f32[512]{0:T(512)S(1)} %select_multiply_fusion.2, s32[1024]{0:T(1024)S(1)} %iota_add_fusion.4, s32[512]{0:T(512)S(1)} %iota_add_fusion.5, f32[192,1024]{1,0:T(8,128)} %get-tuple-element.190, pred[]{:T(512)S(6)} %compare.4, bf16[192,8192]{1,0:T(8,128)(2,1)} %get-tuple-element.199, ...), kind=kOutput, calls=%fused_computation.13.clone.1 | convolution fusion | flops 210108416 | bytes 1777669 | tf_op jit(solution)/shard_map/while/body/eval_jaxpr/dot_general | solution.py:35
  413.1 9.0 %convolution_add_fusion.5 = f32[192,1024]{1,0:T(8,128)} fusion(f32[192,1024]{1,0:T(8,128)S(1)} %convolution_add_fusion.4, f32[512]{0:T(512)S(1)} %select_multiply_fusion.2, s32[1024]{0:T(1024)S(1)} %iota_add_fusion.4, s32[512]{0:T(512)S(1)} %iota_add_fusion.5, bf16[192,8192]{1,0:T(8,128)(2,1)S(1)} %get-tuple-element.200, s32[]{:T(128)S(6)} %select_n.93), kind=kOutput, calls=%fused_computation.12.clone.1 | convolution fusion | flops 210436096 | bytes 1777668 | tf_op jit(solution)/shard_map/while/body/eval_jaxpr/dot_general | solution.py:36
  422.1 9.2 %convolution_add_fusion.4 = f32[192,1024]{1,0:T(8,128)S(1)} fusion(f32[512]{0:T(512)S(1)} %select_multiply_fusion.2, s32[1024]{0:T(1024)S(1)} %iota_add_fusion.4, s32[512]{0:T(512)S(1)} %iota_add_fusion.5, f32[192,1024]{1,0:T(8,128)} %get-tuple-element.190, pred[]{:T(512)S(6)} %compare.4, bf16[192,8192]{1,0:T(8,128)(2,1)} %get-tuple-element.199, ...), kind=kOutput, calls=%fused_computation.13.clone.1 | convolution fusion | flops 210108416 | bytes 1777669 | tf_op jit(solution)/shard_map/while/body/eval_jaxpr/dot_general | solution.py:35
  431.3 9.0 %convolution_add_fusion.5 = f32[192,1024]{1,0:T(8,128)} fusion(f32[192,1024]{1,0:T(8,128)S(1)} %convolution_add_fusion.4, f32[512]{0:T(512)S(1)} %select_multiply_fusion.2, s32[1024]{0:T(1024)S(1)} %iota_add_fusion.4, s32[512]{0:T(512)S(1)} %iota_add_fusion.5, bf16[192,8192]{1,0:T(8,128)(2,1)S(1)} %get-tuple-element.200, s32[]{:T(128)S(6)} %select_n.93), kind=kOutput, calls=%fused_computation.12.clone.1 | convolution fusion | flops 210436096 | bytes 1777668 | tf_op jit(solution)/shard_map/while/body/eval_jaxpr/dot_general | solution.py:36
  440.2 9.2 %convolution_add_fusion.4 = f32[192,1024]{1,0:T(8,128)S(1)} fusion(f32[512]{0:T(512)S(1)} %select_multiply_fusion.2, s32[1024]{0:T(1024)S(1)} %iota_add_fusion.4, s32[512]{0:T(512)S(1)} %iota_add_fusion.5, f32[192,1024]{1,0:T(8,128)} %get-tuple-element.190, pred[]{:T(512)S(6)} %compare.4, bf16[192,8192]{1,0:T(8,128)(2,1)} %get-tuple-element.199, ...), kind=kOutput, calls=%fused_computation.13.clone.1 | convolution fusion | flops 210108416 | bytes 1777669 | tf_op jit(solution)/shard_map/while/body/eval_jaxpr/dot_general | solution.py:35
  458.4 9.2 %convolution_add_fusion.4 = f32[192,1024]{1,0:T(8,128)S(1)} fusion(f32[512]{0:T(512)S(1)} %select_multiply_fusion.2, s32[1024]{0:T(1024)S(1)} %iota_add_fusion.4, s32[512]{0:T(512)S(1)} %iota_add_fusion.5, f32[192,1024]{1,0:T(8,128)} %get-tuple-element.190, pred[]{:T(512)S(6)} %compare.4, bf16[192,8192]{1,0:T(8,128)(2,1)} %get-tuple-element.199, ...), kind=kOutput, calls=%fused_computation.13.clone.1 | convolution fusion | flops 210108416 | bytes 1777669 | tf_op jit(solution)/shard_map/while/body/eval_jaxpr/dot_general | solution.py:35
  476.6 9.2 %convolution_add_fusion.4 = f32[192,1024]{1,0:T(8,128)S(1)} fusion(f32[512]{0:T(512)S(1)} %select_multiply_fusion.2, s32[1024]{0:T(1024)S(1)} %iota_add_fusion.4, s32[512]{0:T(512)S(1)} %iota_add_fusion.5, f32[192,1024]{1,0:T(8,128)} %get-tuple-element.190, pred[]{:T(512)S(6)} %compare.4, bf16[192,8192]{1,0:T(8,128)(2,1)} %get-tuple-element.199, ...), kind=kOutput, calls=%fused_computation.13.clone.1 | convolution fusion | flops 210108416 | bytes 1777669 | tf_op jit(solution)/shard_map/while/body/eval_jaxpr/dot_general | solution.py:35
  494.7 9.2 %convolution_add_fusion.4 = f32[192,1024]{1,0:T(8,128)S(1)} fusion(f32[512]{0:T(512)S(1)} %select_multiply_fusion.2, s32[1024]{0:T(1024)S(1)} %iota_add_fusion.4, s32[512]{0:T(512)S(1)} %iota_add_fusion.5, f32[192,1024]{1,0:T(8,128)} %get-tuple-element.190, pred[]{:T(512)S(6)} %compare.4, bf16[192,8192]{1,0:T(8,128)(2,1)} %get-tuple-element.199, ...), kind=kOutput, calls=%fused_computation.13.clone.1 | convolution fusion | flops 210108416 | bytes 1777669 | tf_op jit(solution)/shard_map/while/body/eval_jaxpr/dot_general | solution.py:35
  512.9 9.2 %convolution_add_fusion.4 = f32[192,1024]{1,0:T(8,128)S(1)} fusion(f32[512]{0:T(512)S(1)} %select_multiply_fusion.2, s32[1024]{0:T(1024)S(1)} %iota_add_fusion.4, s32[512]{0:T(512)S(1)} %iota_add_fusion.5, f32[192,1024]{1,0:T(8,128)} %get-tuple-element.190, pred[]{:T(512)S(6)} %compare.4, bf16[192,8192]{1,0:T(8,128)(2,1)} %get-tuple-element.199, ...), kind=kOutput, calls=%fused_computation.13.clone.1 | convolution fusion | flops 210108416 | bytes 1777669 | tf_op jit(solution)/shard_map/while/body/eval_jaxpr/dot_general | solution.py:35
  531.0 9.2 %convolution_add_fusion.4 = f32[192,1024]{1,0:T(8,128)S(1)} fusion(f32[512]{0:T(512)S(1)} %select_multiply_fusion.2, s32[1024]{0:T(1024)S(1)} %iota_add_fusion.4, s32[512]{0:T(512)S(1)} %iota_add_fusion.5, f32[192,1024]{1,0:T(8,128)} %get-tuple-element.190, pred[]{:T(512)S(6)} %compare.4, bf16[192,8192]{1,0:T(8,128)(2,1)} %get-tuple-element.199, ...), kind=kOutput, calls=%fused_computation.13.clone.1 | convolution fusion | flops 210108416 | bytes 1777669 | tf_op jit(solution)/shard_map/while/body/eval_jaxpr/dot_general | solution.py:35
  549.2 9.2 %convolution_add_fusion.4 = f32[192,1024]{1,0:T(8,128)S(1)} fusion(f32[512]{0:T(512)S(1)} %select_multiply_fusion.2, s32[1024]{0:T(1024)S(1)} %iota_add_fusion.4, s32[512]{0:T(512)S(1)} %iota_add_fusion.5, f32[192,1024]{1,0:T(8,128)} %get-tuple-element.190, pred[]{:T(512)S(6)} %compare.4, bf16[192,8192]{1,0:T(8,128)(2,1)} %get-tuple-element.199, ...), kind=kOutput, calls=%fused_computation.13.clone.1 | convolution fusion | flops 210108416 | bytes 1777669 | tf_op jit(solution)/shard_map/while/body/eval_jaxpr/dot_general | solution.py:35
  567.3 9.2 %convolution_add_fusion.4 = f32[192,1024]{1,0:T(8,128)S(1)} fusion(f32[512]{0:T(512)S(1)} %select_multiply_fusion.2, s32[1024]{0:T(1024)S(1)} %iota_add_fusion.4, s32[512]{0:T(512)S(1)} %iota_add_fusion.5, f32[192,1024]{1,0:T(8,128)} %get-tuple-element.190, pred[]{:T(512)S(6)} %compare.4, bf16[192,8192]{1,0:T(8,128)(2,1)} %get-tuple-element.199, ...), kind=kOutput, calls=%fused_computation.13.clone.1 | convolution fusion | flops 210108416 | bytes 1777669 | tf_op jit(solution)/shard_map/while/body/eval_jaxpr/dot_general | solution.py:35
  576.5 9.0 %convolution_add_fusion.5 = f32[192,1024]{1,0:T(8,128)} fusion(f32[192,1024]{1,0:T(8,128)S(1)} %convolution_add_fusion.4, f32[512]{0:T(512)S(1)} %select_multiply_fusion.2, s32[1024]{0:T(1024)S(1)} %iota_add_fusion.4, s32[512]{0:T(512)S(1)} %iota_add_fusion.5, bf16[192,8192]{1,0:T(8,128)(2,1)S(1)} %get-tuple-element.200, s32[]{:T(128)S(6)} %select_n.93), kind=kOutput, calls=%fused_computation.12.clone.1 | convolution fusion | flops 210436096 | bytes 1777668 | tf_op jit(solution)/shard_map/while/body/eval_jaxpr/dot_general | solution.py:36
  585.5 9.2 %convolution_add_fusion.4 = f32[192,1024]{1,0:T(8,128)S(1)} fusion(f32[512]{0:T(512)S(1)} %select_multiply_fusion.2, s32[1024]{0:T(1024)S(1)} %iota_add_fusion.4, s32[512]{0:T(512)S(1)} %iota_add_fusion.5, f32[192,1024]{1,0:T(8,128)} %get-tuple-element.190, pred[]{:T(512)S(6)} %compare.4, bf16[192,8192]{1,0:T(8,128)(2,1)} %get-tuple-element.199, ...), kind=kOutput, calls=%fused_computation.13.clone.1 | convolution fusion | flops 210108416 | bytes 1777669 | tf_op jit(solution)/shard_map/while/body/eval_jaxpr/dot_general | solution.py:35
  603.6 9.2 %convolution_add_fusion.4 = f32[192,1024]{1,0:T(8,128)S(1)} fusion(f32[512]{0:T(512)S(1)} %select_multiply_fusion.2, s32[1024]{0:T(1024)S(1)} %iota_add_fusion.4, s32[512]{0:T(512)S(1)} %iota_add_fusion.5, f32[192,1024]{1,0:T(8,128)} %get-tuple-element.190, pred[]{:T(512)S(6)} %compare.4, bf16[192,8192]{1,0:T(8,128)(2,1)} %get-tuple-element.199, ...), kind=kOutput, calls=%fused_computation.13.clone.1 | convolution fusion | flops 210108416 | bytes 1777669 | tf_op jit(solution)/shard_map/while/body/eval_jaxpr/dot_general | solution.py:35
  612.8 9.0 %convolution_add_fusion.5 = f32[192,1024]{1,0:T(8,128)} fusion(f32[192,1024]{1,0:T(8,128)S(1)} %convolution_add_fusion.4, f32[512]{0:T(512)S(1)} %select_multiply_fusion.2, s32[1024]{0:T(1024)S(1)} %iota_add_fusion.4, s32[512]{0:T(512)S(1)} %iota_add_fusion.5, bf16[192,8192]{1,0:T(8,128)(2,1)S(1)} %get-tuple-element.200, s32[]{:T(128)S(6)} %select_n.93), kind=kOutput, calls=%fused_computation.12.clone.1 | convolution fusion | flops 210436096 | bytes 1777668 | tf_op jit(solution)/shard_map/while/body/eval_jaxpr/dot_general | solution.py:36
  621.8 9.2 %convolution_add_fusion.4 = f32[192,1024]{1,0:T(8,128)S(1)} fusion(f32[512]{0:T(512)S(1)} %select_multiply_fusion.2, s32[1024]{0:T(1024)S(1)} %iota_add_fusion.4, s32[512]{0:T(512)S(1)} %iota_add_fusion.5, f32[192,1024]{1,0:T(8,128)} %get-tuple-element.190, pred[]{:T(512)S(6)} %compare.4, bf16[192,8192]{1,0:T(8,128)(2,1)} %get-tuple-element.199, ...), kind=kOutput, calls=%fused_computation.13.clone.1 | convolution fusion | flops 210108416 | bytes 1777669 | tf_op jit(solution)/shard_map/while/body/eval_jaxpr/dot_general | solution.py:35
  640.0 9.2 %convolution_add_fusion.4 = f32[192,1024]{1,0:T(8,128)S(1)} fusion(f32[512]{0:T(512)S(1)} %select_multiply_fusion.2, s32[1024]{0:T(1024)S(1)} %iota_add_fusion.4, s32[512]{0:T(512)S(1)} %iota_add_fusion.5, f32[192,1024]{1,0:T(8,128)} %get-tuple-element.190, pred[]{:T(512)S(6)} %compare.4, bf16[192,8192]{1,0:T(8,128)(2,1)} %get-tuple-element.199, ...), kind=kOutput, calls=%fused_computation.13.clone.1 | convolution fusion | flops 210108416 | bytes 1777669 | tf_op jit(solution)/shard_map/while/body/eval_jaxpr/dot_general | solution.py:35
  649.1 9.0 %convolution_add_fusion.5 = f32[192,1024]{1,0:T(8,128)} fusion(f32[192,1024]{1,0:T(8,128)S(1)} %convolution_add_fusion.4, f32[512]{0:T(512)S(1)} %select_multiply_fusion.2, s32[1024]{0:T(1024)S(1)} %iota_add_fusion.4, s32[512]{0:T(512)S(1)} %iota_add_fusion.5, bf16[192,8192]{1,0:T(8,128)(2,1)S(1)} %get-tuple-element.200, s32[]{:T(128)S(6)} %select_n.93), kind=kOutput, calls=%fused_computation.12.clone.1 | convolution fusion | flops 210436096 | bytes 1777668 | tf_op jit(solution)/shard_map/while/body/eval_jaxpr/dot_general | solution.py:36
  658.1 9.2 %convolution_add_fusion.4 = f32[192,1024]{1,0:T(8,128)S(1)} fusion(f32[512]{0:T(512)S(1)} %select_multiply_fusion.2, s32[1024]{0:T(1024)S(1)} %iota_add_fusion.4, s32[512]{0:T(512)S(1)} %iota_add_fusion.5, f32[192,1024]{1,0:T(8,128)} %get-tuple-element.190, pred[]{:T(512)S(6)} %compare.4, bf16[192,8192]{1,0:T(8,128)(2,1)} %get-tuple-element.199, ...), kind=kOutput, calls=%fused_computation.13.clone.1 | convolution fusion | flops 210108416 | bytes 1777669 | tf_op jit(solution)/shard_map/while/body/eval_jaxpr/dot_general | solution.py:35
  (108 shorter events, 155.6 us)
Async XLA Ops:
  6.5 58.1 %all-gather.2.cloned.1.call-start = ((), (), s32[]{:S(2)}) async-start(), calls=%async_computation.2 | async-start | bytes 9437184 | tf_op jit(solution)/shard_map/all_gather | solution.py:65
  8.4 1.2 copy-start.3
  9.6 2.8 copy-start.4
  9.6 3.5 copy-start.5
  109.0 3.1 copy-start.2
  110.6 2.0 copy-start.1
  114.2 2.2 copy-start
  127.5 111.0 %all-to-all-start = ((bf16[16,3,4,2,8192]{4,3,2,1,0:T(2,128)(2,1)}), bf16[16,3,4,2,8192]{4,3,2,1,0:T(2,128)(2,1)}, u32[]{:S(2)}, u32[]{:S(2)}) async-start(bf16[16,3,4,2,8192]{4,3,2,1,0:T(2,128)(2,1)} %bitcast.52), calls=%async_computation | async-start | bytes 12582912 | tf_op jit(solution)/shard_map/all_to_all | solution.py:88
  238.5 114.2 %all-to-all-start.1 = ((bf16[16,3,4,2,8192]{4,3,2,1,0:T(2,128)(2,1)}), bf16[16,3,4,2,8192]{4,3,2,1,0:T(2,128)(2,1)}, u32[]{:S(2)}, u32[]{:S(2)}) async-start(bf16[16,3,4,2,8192]{4,3,2,1,0:T(2,128)(2,1)} %bitcast.51), calls=%async_computation.1 | async-start | bytes 12582912 | tf_op jit(solution)/shard_map/all_to_all | solution.py:88
Sparse Core Ops, SparseCore 0:
  12.5 52.0 all-gather.1
where the time goes:
time: 689 us; the launch traced here: 686 us
  matrix products  295 us (43%)
  waiting for transfers between devices  241 us (35%)
  local copies, waits for them, and re-layouts  93.2 us (14%)
  starting transfers between devices  21.5 us (3%)
  other arithmetic  20.5 us (3%)
  between operations  13.8 us (2%)
    all_to_all x2, waiting for transfers between devices, local(): lax.all_to_all(placed.astype(jnp.bfloat16).reshape(groups_count, MOST, pa...  189 us
    dot_general x16, matrix products, add_block(): jnp.dot(real_slice, cos_part, preferred_element_type=jnp.float32)  146 us
    dot_general x16, matrix products, add_block(): jnp.dot(imag_slice, sin_part, preferred_element_type=jnp.float32)  143 us
    all_gather x1, waiting for transfers between devices, local(): panel = lax.all_gather(white, 'chan', axis=0, tiled=True)  51.4 us
    convert_element_type x2, local copies, waits for them, and re-layouts, local(): placed.astype(jnp.bfloat16).reshape(groups_count, MOST, pairs, 2, F)  22 us
    all_to_all x2, starting transfers between devices, local(): lax.all_to_all(placed.astype(jnp.bfloat16).reshape(groups_count, MOST, pa...  21.5 us
  transfers between devices with their start and end apart: 3, of which 3 were waited for; matrix products, arithmetic and copies ran while one was open for 2% of the time, Pallas kernels for 0%

commit v1 on v0

--- a/solution.py
+++ b/solution.py
@@ -62,7 +62,21 @@
     groups_count = lax.axis_size("grp")
     slot_count = groups_count * MOST
     white = whiten(spectra)
-    panel = lax.all_gather(white, "chan", axis=0, tiled=True)
+    workers = lax.axis_size("chan")
+    parts_seen = []
+    for dev in range(workers):
+        parts_seen.append((dev, (dev + 1) % workers))
+    in_order = []
+    for dev in range(workers):
+        in_order.append((dev, (dev - 1) % workers))
+    local_out, seen_now = ([white], [white])
+    for _ in range(workers // 2):
+        local_out.append(lax.ppermute(local_out[-1], axis_name="chan", perm=parts_seen))
+    for _ in range((workers - 1) // 2):
+        f_now = lax.ppermute(seen_now[-1], axis_name="chan", perm=in_order)
+        seen_now.append(f_now)
+    carry = jnp.concatenate([*local_out[::-1], *seen_now[1:]], 0)
+    panel = jnp.roll(carry, (lax.axis_index("chan") - workers // 2) * white.shape[0], 0)
     blocks = pair_blocks[0, 0]
     offsets = jnp.arange(BLK, dtype=jnp.int32)
     left_idx = blocks[:, 0][:, None] * BLK + offsets

time: 689 us -> 738 us (1.071)
  the two profiles are of different devices: /device:TPU:20 before, /device:TPU:124 now
where the time goes in v1:
time: 738 us; the launch traced here: 730 us
  matrix products  295 us (40%)
  waiting for transfers between devices  243 us (33%)
  local copies, waits for them, and re-layouts  140 us (19%)
  starting transfers between devices  27.1 us (4%)
  other arithmetic  23.5 us (3%)
    all_to_all x2, waiting for transfers between devices, local(): lax.all_to_all(placed.astype(jnp.bfloat16).reshape(groups_count, MOST, pa...  192 us
    dot_general x16, matrix products, add_block(): jnp.dot(real_slice, cos_part, preferred_element_type=jnp.float32)  146 us
    dot_general x16, matrix products, add_block(): jnp.dot(imag_slice, sin_part, preferred_element_type=jnp.float32)  143 us
    ppermute x4, waiting for transfers between devices, local(): lax.ppermute(local_out[-1], axis_name='chan', perm=parts_seen)  51.2 us
    unnamed x31, local copies, waits for them, and re-layouts  33.8 us
    dynamic_slice x2, local copies, waits for them, and re-layouts, local(): jnp.roll(carry, (lax.axis_index('chan') - workers // 2) * white.shape[0], 0)  23.9 us
    convert_element_type x2, local copies, waits for them, and re-layouts, local(): placed.astype(jnp.bfloat16).reshape(groups_count, MOST, pairs, 2, F)  22 us
    all_to_all x2, starting transfers between devices, local(): lax.all_to_all(placed.astype(jnp.bfloat16).reshape(groups_count, MOST, pa...  21.9 us
  transfers between devices with their start and end apart: 9, of which 6 were waited for; matrix products, arithmetic and copies ran while one was open for 4% of the time, Pallas kernels for 0%

profile of v1, /device:TPU:124, one launch (start us, length us, event | category | flops | bytes accessed | tf_op | source)
XLA Modules:
  0.0 730.4 jit_solution(1469261591629827362)
XLA Ops:
  3.7 14.2 %collective-permute-done = bf16[16,2,2,8192]{3,0,2,1:T(8,128)(2,1)S(1)} collective-permute-done((bf16[16,2,2,8192]{3,0,2,1:T(8,128)(2,1)S(1)}, bf16[16,2,2,8192]{3,0,2,1:T(8,128)(2,1)S(1)}, u32[]{:S(2)}, u32[]{:S(2)}) %collective-permute-start) | collective-permute-done | bytes 1048608 | tf_op jit(solution)/shard_map/ppermute | solution.py:74
  19.7 12.5 %collective-permute-done.1 = bf16[16,2,2,8192]{3,0,2,1:T(8,128)(2,1)S(1)} collective-permute-done((bf16[16,2,2,8192]{3,0,2,1:T(8,128)(2,1)S(1)}, bf16[16,2,2,8192]{3,0,2,1:T(8,128)(2,1)S(1)}, u32[]{:S(2)}, u32[]{:S(2)}) %collective-permute-start.1) | collective-permute-done | bytes 1048608 | tf_op jit(solution)/shard_map/ppermute | solution.py:74
  34.9 12.6 %collective-permute-done.2 = bf16[16,2,2,8192]{3,0,2,1:T(8,128)(2,1)} collective-permute-done((bf16[16,2,2,8192]{3,0,2,1:T(8,128)(2,1)S(1)}, bf16[16,2,2,8192]{3,0,2,1:T(8,128)(2,1)}, u32[]{:S(2)}, u32[]{:S(2)}) %collective-permute-start.2) | collective-permute-done | bytes 1048608 | tf_op jit(solution)/shard_map/ppermute | solution.py:74
  50.1 11.9 %collective-permute-done.3 = bf16[16,2,2,8192]{3,0,2,1:T(8,128)(2,1)} collective-permute-done((bf16[16,2,2,8192]{3,0,2,1:T(8,128)(2,1)}, bf16[16,2,2,8192]{3,0,2,1:T(8,128)(2,1)}, u32[]{:S(2)}, u32[]{:S(2)}) %collective-permute-start.3) | collective-permute-done | bytes 1048608 | tf_op jit(solution)/shard_map/ppermute | solution.py:74
  96.9 16.3 %copy.41 = bf16[128,2,2,8192]{3,2,1,0:T(2,128)(2,1)} copy(bf16[128,2,2,8192]{3,0,2,1:T(8,128)(2,1)} %constant_dynamic-slice_fusion) | data formatting | bytes 16777216 | tf_op jit(solution)/shard_map/jit(_roll_dynamic)/dynamic_slice | solution.py:79
  113.2 11.3 %gather_fusion = bf16[36,2,2,8192]{3,2,1,0:T(2,128)(2,1)S(1)} fusion(bf16[128,2,2,8192]{3,2,1,0:T(2,128)(2,1)} %copy.41, s32[1024]{0:T(1024)S(1)} %pad_clamp_fusion.1), kind=kCustom, calls=%fused_computation.clone | custom fusion | bytes 4718736 | tf_op jit(solution)/shard_map/jit(_take)/gather | solution.py:84
  138.6 11.5 %gather_fusion.1 = bf16[36,2,2,8192]{3,2,1,0:T(2,128)(2,1)S(1)} fusion(bf16[128,2,2,8192]{3,2,1,0:T(2,128)(2,1)} %copy.41, s32[1024]{0:T(1024)S(1)} %pad_clamp_fusion), kind=kCustom, calls=%fused_computation.1.clone | custom fusion | bytes 4718736 | tf_op jit(solution)/shard_map/jit(_take)/gather | solution.py:85
  164.9 11.0 %copy.49 = bf16[48,4,2,8192]{3,2,1,0:T(2,128)(2,1)} copy(bf16[48,4,2,8192]{3,0,2,1:T(8,128)(2,1)S(1)} %convolution_convert_fusion.1) | data formatting | bytes 12582912 | tf_op jit(solution)/shard_map/convert_element_type | solution.py:103
  186.3 11.0 %copy.50 = bf16[48,4,2,8192]{3,2,1,0:T(2,128)(2,1)} copy(bf16[48,4,2,8192]{3,0,2,1:T(8,128)(2,1)S(1)} %convolution_convert_fusion) | data formatting | bytes 12582912 | tf_op jit(solution)/shard_map/convert_element_type | solution.py:103
  197.3 86.1 %all-to-all-done = bf16[16,3,4,2,8192]{4,3,2,1,0:T(2,128)(2,1)} async-done(((bf16[16,3,4,2,8192]{4,3,2,1,0:T(2,128)(2,1)}), bf16[16,3,4,2,8192]{4,3,2,1,0:T(2,128)(2,1)}, u32[]{:S(2)}, u32[]{:S(2)}) %all-to-all-start) | async-done | bytes 6291488 | tf_op jit(solution)/shard_map/all_to_all | solution.py:102
  283.5 14.8 %all-to-all-start.1 = ((bf16[16,3,4,2,8192]{4,3,2,1,0:T(2,128)(2,1)}), bf16[16,3,4,2,8192]{4,3,2,1,0:T(2,128)(2,1)}, u32[]{:S(2)}, u32[]{:S(2)}) async-start(bf16[16,3,4,2,8192]{4,3,2,1,0:T(2,128)(2,1)} %bitcast.51), calls=%async_computation.1 | async-start | bytes 12582912 | tf_op jit(solution)/shard_map/all_to_all | solution.py:102
  298.2 106.0 %all-to-all-done.1 = bf16[16,3,4,2,8192]{4,3,2,1,0:T(2,128)(2,1)} async-done(((bf16[16,3,4,2,8192]{4,3,2,1,0:T(2,128)(2,1)}), bf16[16,3,4,2,8192]{4,3,2,1,0:T(2,128)(2,1)}, u32[]{:S(2)}, u32[]{:S(2)}) %all-to-all-start.1) | async-done | bytes 6291488 | tf_op jit(solution)/shard_map/all_to_all | solution.py:102
  404.3 11.2 %multiply_convert_fusion.4 = bf16[16,3,4,2,8192]{4,3,2,1,0:T(2,128)(2,1)S(1)} fusion(bf16[16,3,4,2,8192]{4,3,2,1,0:T(2,128)(2,1)} %all-to-all-done.1, bf16[16,3,4,2,8192]{4,3,2,1,0:T(2,128)(2,1)} %all-to-all-done), kind=kLoop, calls=%fused_computation.29 | loop fusion | flops 15728640 | bytes 18874368 | tf_op jit(solution)/shard_map/convert_element_type | solution.py:109
  415.4 13.4 %fusion.35 = (bf16[192,1,8192]{2,1,0:T(2,128)(2,1)S(1)}, bf16[192,1,8192]{2,1,0:T(2,128)(2,1)S(1)}) fusion(bf16[192,2,8192]{2,1,0:T(2,128)(2,1)S(1)} %bitcast.46), kind=kLoop, calls=%fused_computation.94 | loop fusion | bytes 12582912 | tf_op jit(solution)/shard_map/slice | solution.py:28
  437.4 290.3 %while.16 = (s32[]{:T(128)}, f32[192,1024]{1,0:T(8,128)}, bf16[192,8192]{1,0:T(8,128)(2,1)}, bf16[192,8192]{1,0:T(8,128)(2,1)S(1)}, s32[]{:T(128)}, /*index=5*/s32[]{:T(128)}, s32[]{:T(128)}, s32[]{:T(128)}) while((s32[]{:T(128)}, f32[192,1024]{1,0:T(8,128)}, bf16[192,8192]{1,0:T(8,128)(2,1)}, bf16[192,8192]{1,0:T(8,128)(2,1)S(1)}, ...), condition=%wide.region_3.5_spmd.clone, body=%wide.region_2.4_spmd.clone.sunk | while | flops 420548096 | bytes 3563677 | solution.py:39
  455.5 9.2 %convolution_add_fusion.4 = f32[192,1024]{1,0:T(8,128)S(1)} fusion(f32[512]{0:T(512)S(1)} %select_multiply_fusion.2, s32[1024]{0:T(1024)S(1)} %iota_add_fusion.4, s32[512]{0:T(512)S(1)} %iota_add_fusion.5, f32[192,1024]{1,0:T(8,128)} %get-tuple-element.190, pred[]{:T(512)S(6)} %compare.5, bf16[192,8192]{1,0:T(8,128)(2,1)} %get-tuple-element.199, ...), kind=kOutput, calls=%fused_computation.13.clone.1 | convolution fusion | flops 210108416 | bytes 1777669 | tf_op jit(solution)/shard_map/while/body/eval_jaxpr/dot_general | solution.py:35
  473.6 9.2 %convolution_add_fusion.4 = f32[192,1024]{1,0:T(8,128)S(1)} fusion(f32[512]{0:T(512)S(1)} %select_multiply_fusion.2, s32[1024]{0:T(1024)S(1)} %iota_add_fusion.4, s32[512]{0:T(512)S(1)} %iota_add_fusion.5, f32[192,1024]{1,0:T(8,128)} %get-tuple-element.190, pred[]{:T(512)S(6)} %compare.5, bf16[192,8192]{1,0:T(8,128)(2,1)} %get-tuple-element.199, ...), kind=kOutput, calls=%fused_computation.13.clone.1 | convolution fusion | flops 210108416 | bytes 1777669 | tf_op jit(solution)/shard_map/while/body/eval_jaxpr/dot_general | solution.py:35
  491.8 9.2 %convolution_add_fusion.4 = f32[192,1024]{1,0:T(8,128)S(1)} fusion(f32[512]{0:T(512)S(1)} %select_multiply_fusion.2, s32[1024]{0:T(1024)S(1)} %iota_add_fusion.4, s32[512]{0:T(512)S(1)} %iota_add_fusion.5, f32[192,1024]{1,0:T(8,128)} %get-tuple-element.190, pred[]{:T(512)S(6)} %compare.5, bf16[192,8192]{1,0:T(8,128)(2,1)} %get-tuple-element.199, ...), kind=kOutput, calls=%fused_computation.13.clone.1 | convolution fusion | flops 210108416 | bytes 1777669 | tf_op jit(solution)/shard_map/while/body/eval_jaxpr/dot_general | solution.py:35
  510.0 9.2 %convolution_add_fusion.4 = f32[192,1024]{1,0:T(8,128)S(1)} fusion(f32[512]{0:T(512)S(1)} %select_multiply_fusion.2, s32[1024]{0:T(1024)S(1)} %iota_add_fusion.4, s32[512]{0:T(512)S(1)} %iota_add_fusion.5, f32[192,1024]{1,0:T(8,128)} %get-tuple-element.190, pred[]{:T(512)S(6)} %compare.5, bf16[192,8192]{1,0:T(8,128)(2,1)} %get-tuple-element.199, ...), kind=kOutput, calls=%fused_computation.13.clone.1 | convolution fusion | flops 210108416 | bytes 1777669 | tf_op jit(solution)/shard_map/while/body/eval_jaxpr/dot_general | solution.py:35
  528.1 9.2 %convolution_add_fusion.4 = f32[192,1024]{1,0:T(8,128)S(1)} fusion(f32[512]{0:T(512)S(1)} %select_multiply_fusion.2, s32[1024]{0:T(1024)S(1)} %iota_add_fusion.4, s32[512]{0:T(512)S(1)} %iota_add_fusion.5, f32[192,1024]{1,0:T(8,128)} %get-tuple-element.190, pred[]{:T(512)S(6)} %compare.5, bf16[192,8192]{1,0:T(8,128)(2,1)} %get-tuple-element.199, ...), kind=kOutput, calls=%fused_computation.13.clone.1 | convolution fusion | flops 210108416 | bytes 1777669 | tf_op jit(solution)/shard_map/while/body/eval_jaxpr/dot_general | solution.py:35
  537.3 9.0 %convolution_add_fusion.5 = f32[192,1024]{1,0:T(8,128)} fusion(f32[192,1024]{1,0:T(8,128)S(1)} %convolution_add_fusion.4, f32[512]{0:T(512)S(1)} %select_multiply_fusion.2, s32[1024]{0:T(1024)S(1)} %iota_add_fusion.4, s32[512]{0:T(512)S(1)} %iota_add_fusion.5, bf16[192,8192]{1,0:T(8,128)(2,1)S(1)} %get-tuple-element.200, s32[]{:T(128)S(6)} %select_n.107), kind=kOutput, calls=%fused_computation.12.clone.1 | convolution fusion | flops 210436096 | bytes 1777668 | tf_op jit(solution)/shard_map/while/body/eval_jaxpr/dot_general | solution.py:36
  546.3 9.2 %convolution_add_fusion.4 = f32[192,1024]{1,0:T(8,128)S(1)} fusion(f32[512]{0:T(512)S(1)} %select_multiply_fusion.2, s32[1024]{0:T(1024)S(1)} %iota_add_fusion.4, s32[512]{0:T(512)S(1)} %iota_add_fusion.5, f32[192,1024]{1,0:T(8,128)} %get-tuple-element.190, pred[]{:T(512)S(6)} %compare.5, bf16[192,8192]{1,0:T(8,128)(2,1)} %get-tuple-element.199, ...), kind=kOutput, calls=%fused_computation.13.clone.1 | convolution fusion | flops 210108416 | bytes 1777669 | tf_op jit(solution)/shard_map/while/body/eval_jaxpr/dot_general | solution.py:35
  564.4 9.2 %convolution_add_fusion.4 = f32[192,1024]{1,0:T(8,128)S(1)} fusion(f32[512]{0:T(512)S(1)} %select_multiply_fusion.2, s32[1024]{0:T(1024)S(1)} %iota_add_fusion.4, s32[512]{0:T(512)S(1)} %iota_add_fusion.5, f32[192,1024]{1,0:T(8,128)} %get-tuple-element.190, pred[]{:T(512)S(6)} %compare.5, bf16[192,8192]{1,0:T(8,128)(2,1)} %get-tuple-element.199, ...), kind=kOutput, calls=%fused_computation.13.clone.1 | convolution fusion | flops 210108416 | bytes 1777669 | tf_op jit(solution)/shard_map/while/body/eval_jaxpr/dot_general | solution.py:35
  573.6 9.0 %convolution_add_fusion.5 = f32[192,1024]{1,0:T(8,128)} fusion(f32[192,1024]{1,0:T(8,128)S(1)} %convolution_add_fusion.4, f32[512]{0:T(512)S(1)} %select_multiply_fusion.2, s32[1024]{0:T(1024)S(1)} %iota_add_fusion.4, s32[512]{0:T(512)S(1)} %iota_add_fusion.5, bf16[192,8192]{1,0:T(8,128)(2,1)S(1)} %get-tuple-element.200, s32[]{:T(128)S(6)} %select_n.107), kind=kOutput, calls=%fused_computation.12.clone.1 | convolution fusion | flops 210436096 | bytes 1777668 | tf_op jit(solution)/shard_map/while/body/eval_jaxpr/dot_general | solution.py:36
  582.6 9.2 %convolution_add_fusion.4 = f32[192,1024]{1,0:T(8,128)S(1)} fusion(f32[512]{0:T(512)S(1)} %select_multiply_fusion.2, s32[1024]{0:T(1024)S(1)} %iota_add_fusion.4, s32[512]{0:T(512)S(1)} %iota_add_fusion.5, f32[192,1024]{1,0:T(8,128)} %get-tuple-element.190, pred[]{:T(512)S(6)} %compare.5, bf16[192,8192]{1,0:T(8,128)(2,1)} %get-tuple-element.199, ...), kind=kOutput, calls=%fused_computation.13.clone.1 | convolution fusion | flops 210108416 | bytes 1777669 | tf_op jit(solution)/shard_map/while/body/eval_jaxpr/dot_general | solution.py:35
  600.7 9.2 %convolution_add_fusion.4 = f32[192,1024]{1,0:T(8,128)S(1)} fusion(f32[512]{0:T(512)S(1)} %select_multiply_fusion.2, s32[1024]{0:T(1024)S(1)} %iota_add_fusion.4, s32[512]{0:T(512)S(1)} %iota_add_fusion.5, f32[192,1024]{1,0:T(8,128)} %get-tuple-element.190, pred[]{:T(512)S(6)} %compare.5, bf16[192,8192]{1,0:T(8,128)(2,1)} %get-tuple-element.199, ...), kind=kOutput, calls=%fused_computation.13.clone.1 | convolution fusion | flops 210108416 | bytes 1777669 | tf_op jit(solution)/shard_map/while/body/eval_jaxpr/dot_general | solution.py:35
  618.9 9.2 %convolution_add_fusion.4 = f32[192,1024]{1,0:T(8,128)S(1)} fusion(f32[512]{0:T(512)S(1)} %select_multiply_fusion.2, s32[1024]{0:T(1024)S(1)} %iota_add_fusion.4, s32[512]{0:T(512)S(1)} %iota_add_fusion.5, f32[192,1024]{1,0:T(8,128)} %get-tuple-element.190, pred[]{:T(512)S(6)} %compare.5, bf16[192,8192]{1,0:T(8,128)(2,1)} %get-tuple-element.199, ...), kind=kOutput, calls=%fused_computation.13.clone.1 | convolution fusion | flops 210108416 | bytes 1777669 | tf_op jit(solution)/shard_map/while/body/eval_jaxpr/dot_general | solution.py:35
  637.0 9.2 %convolution_add_fusion.4 = f32[192,1024]{1,0:T(8,128)S(1)} fusion(f32[512]{0:T(512)S(1)} %select_multiply_fusion.2, s32[1024]{0:T(1024)S(1)} %iota_add_fusion.4, s32[512]{0:T(512)S(1)} %iota_add_fusion.5, f32[192,1024]{1,0:T(8,128)} %get-tuple-element.190, pred[]{:T(512)S(6)} %compare.5, bf16[192,8192]{1,0:T(8,128)(2,1)} %get-tuple-element.199, ...), kind=kOutput, calls=%fused_computation.13.clone.1 | convolution fusion | flops 210108416 | bytes 1777669 | tf_op jit(solution)/shard_map/while/body/eval_jaxpr/dot_general | solution.py:35
  655.2 9.2 %convolution_add_fusion.4 = f32[192,1024]{1,0:T(8,128)S(1)} fusion(f32[512]{0:T(512)S(1)} %select_multiply_fusion.2, s32[1024]{0:T(1024)S(1)} %iota_add_fusion.4, s32[512]{0:T(512)S(1)} %iota_add_fusion.5, f32[192,1024]{1,0:T(8,128)} %get-tuple-element.190, pred[]{:T(512)S(6)} %compare.5, bf16[192,8192]{1,0:T(8,128)(2,1)} %get-tuple-element.199, ...), kind=kOutput, calls=%fused_computation.13.clone.1 | convolution fusion | flops 210108416 | bytes 1777669 | tf_op jit(solution)/shard_map/while/body/eval_jaxpr/dot_general | solution.py:35
  673.3 9.2 %convolution_add_fusion.4 = f32[192,1024]{1,0:T(8,128)S(1)} fusion(f32[512]{0:T(512)S(1)} %select_multiply_fusion.2, s32[1024]{0:T(1024)S(1)} %iota_add_fusion.4, s32[512]{0:T(512)S(1)} %iota_add_fusion.5, f32[192,1024]{1,0:T(8,128)} %get-tuple-element.190, pred[]{:T(512)S(6)} %compare.5, bf16[192,8192]{1,0:T(8,128)(2,1)} %get-tuple-element.199, ...), kind=kOutput, calls=%fused_computation.13.clone.1 | convolution fusion | flops 210108416 | bytes 1777669 | tf_op jit(solution)/shard_map/while/body/eval_jaxpr/dot_general | solution.py:35
  691.5 9.2 %convolution_add_fusion.4 = f32[192,1024]{1,0:T(8,128)S(1)} fusion(f32[512]{0:T(512)S(1)} %select_multiply_fusion.2, s32[1024]{0:T(1024)S(1)} %iota_add_fusion.4, s32[512]{0:T(512)S(1)} %iota_add_fusion.5, f32[192,1024]{1,0:T(8,128)} %get-tuple-element.190, pred[]{:T(512)S(6)} %compare.5, bf16[192,8192]{1,0:T(8,128)(2,1)} %get-tuple-element.199, ...), kind=kOutput, calls=%fused_computation.13.clone.1 | convolution fusion | flops 210108416 | bytes 1777669 | tf_op jit(solution)/shard_map/while/body/eval_jaxpr/dot_general | solution.py:35
  709.6 9.2 %convolution_add_fusion.4 = f32[192,1024]{1,0:T(8,128)S(1)} fusion(f32[512]{0:T(512)S(1)} %select_multiply_fusion.2, s32[1024]{0:T(1024)S(1)} %iota_add_fusion.4, s32[512]{0:T(512)S(1)} %iota_add_fusion.5, f32[192,1024]{1,0:T(8,128)} %get-tuple-element.190, pred[]{:T(512)S(6)} %compare.5, bf16[192,8192]{1,0:T(8,128)(2,1)} %get-tuple-element.199, ...), kind=kOutput, calls=%fused_computation.13.clone.1 | convolution fusion | flops 210108416 | bytes 1777669 | tf_op jit(solution)/shard_map/while/body/eval_jaxpr/dot_general | solution.py:35
  (140 shorter events, 230.0 us)
Async XLA Ops:
  1.8 1.2 copy-start.1
  2.1 45.4 %copy-start.6 = (s32[1,1,18,2]{2,3,1,0:T(2,128)S(1)}, s32[1,1,18,2]{2,3,1,0:T(2,128)}, u32[]{:S(2)}) copy-start(s32[1,1,18,2]{2,3,1,0:T(2,128)} %param.8) | copy-start | bytes 436
  2.1 46.1 %copy-start.7 = (s32[1,1,18,1]{2,3,1,0:T(1,128)S(1)}, s32[1,1,18,1]{2,3,1,0:T(1,128)}, u32[]{:S(2)}) copy-start(s32[1,1,18,1]{2,3,1,0:T(1,128)} %param.9) | copy-start | bytes 220
  3.7 14.2 %collective-permute-start = (bf16[16,2,2,8192]{3,0,2,1:T(8,128)(2,1)S(1)}, bf16[16,2,2,8192]{3,0,2,1:T(8,128)(2,1)S(1)}, u32[]{:S(2)}, u32[]{:S(2)}) collective-permute-start(bf16[16,2,2,8192]{3,0,2,1:T(8,128)(2,1)S(1)} %multiply_convert_fusion.5), channel_id=1, source_target_pairs={{0,1},{1,2},{2,3},{3,4},{4,5},{5,6},{6,7},{7,0},{8,9},{9,10},{10,1... | collective-permute-start | bytes 3145736 | tf_op jit(solution)/shard_map/ppermute | solution.py:74
  17.9 14.2 %collective-permute-start.1 = (bf16[16,2,2,8192]{3,0,2,1:T(8,128)(2,1)S(1)}, bf16[16,2,2,8192]{3,0,2,1:T(8,128)(2,1)S(1)}, u32[]{:S(2)}, u32[]{:S(2)}) collective-permute-start(bf16[16,2,2,8192]{3,0,2,1:T(8,128)(2,1)S(1)} %collective-permute-done), channel_id=1, source_target_pairs={{0,1},{1,2},{2,3},{3,4},{4,5},{5,6},{6,7},{7,0},{8,9},{9,10},{10,1... | collective-permute-start | bytes 3145736 | tf_op jit(solution)/shard_map/ppermute | solution.py:74
  17.9 15.2 %collective-permute-start.4 = (bf16[16,2,2,8192]{3,0,2,1:T(8,128)(2,1)S(1)}, bf16[16,2,2,8192]{3,0,2,1:T(8,128)(2,1)}, u32[]{:S(2)}, u32[]{:S(2)}) collective-permute-start(bf16[16,2,2,8192]{3,0,2,1:T(8,128)(2,1)S(1)} %multiply_convert_fusion.5), channel_id=1, source_target_pairs={{0,7},{1,0},{2,1},{3,2},{4,3},{5,4},{6,5},{7,6},{8,15},{9,8},{10,9... | collective-permute-start | bytes 3145736 | tf_op jit(solution)/shard_map/ppermute | solution.py:76
  32.2 1.0 copy-start.4
  33.1 14.3 %collective-permute-start.2 = (bf16[16,2,2,8192]{3,0,2,1:T(8,128)(2,1)S(1)}, bf16[16,2,2,8192]{3,0,2,1:T(8,128)(2,1)}, u32[]{:S(2)}, u32[]{:S(2)}) collective-permute-start(bf16[16,2,2,8192]{3,0,2,1:T(8,128)(2,1)S(1)} %collective-permute-done.1), channel_id=1, source_target_pairs={{0,1},{1,2},{2,3},{3,4},{4,5},{5,6},{6,7},{7,0},{8,9},{9,10},{10,1... | collective-permute-start | bytes 3145736 | tf_op jit(solution)/shard_map/ppermute | solution.py:74
  33.1 15.2 %collective-permute-start.5 = (bf16[16,2,2,8192]{3,0,2,1:T(8,128)(2,1)}, bf16[16,2,2,8192]{3,0,2,1:T(8,128)(2,1)}, u32[]{:S(2)}, u32[]{:S(2)}) collective-permute-start(bf16[16,2,2,8192]{3,0,2,1:T(8,128)(2,1)} %collective-permute-done.4), channel_id=1, source_target_pairs={{0,7},{1,0},{2,1},{3,2},{4,3},{5,4},{6,5},{7,6},{8,15},{9,8},{10,9... | collective-permute-start | bytes 3145736 | tf_op jit(solution)/shard_map/ppermute | solution.py:76
  47.5 14.5 %collective-permute-start.3 = (bf16[16,2,2,8192]{3,0,2,1:T(8,128)(2,1)}, bf16[16,2,2,8192]{3,0,2,1:T(8,128)(2,1)}, u32[]{:S(2)}, u32[]{:S(2)}) collective-permute-start(bf16[16,2,2,8192]{3,0,2,1:T(8,128)(2,1)} %collective-permute-done.2), channel_id=1, source_target_pairs={{0,1},{1,2},{2,3},{3,4},{4,5},{5,6},{6,7},{7,0},{8,9},{9,10},{10,1... | collective-permute-start | bytes 3145736 | tf_op jit(solution)/shard_map/ppermute | solution.py:74
  48.1 18.4 %copy-start.5 = (bf16[16,2,2,8192]{3,0,2,1:T(8,128)(2,1)S(1)}, bf16[16,2,2,8192]{3,0,2,1:T(8,128)(2,1)}, u32[]{:S(2)}) copy-start(bf16[16,2,2,8192]{3,0,2,1:T(8,128)(2,1)} %copy-done.4) | copy-start | bytes 3145732
  48.4 26.2 %collective-permute-start.6 = (bf16[16,2,2,8192]{3,0,2,1:T(8,128)(2,1)}, bf16[16,2,2,8192]{3,0,2,1:T(8,128)(2,1)S(1)}, u32[]{:S(2)}, u32[]{:S(2)}) collective-permute-start(bf16[16,2,2,8192]{3,0,2,1:T(8,128)(2,1)} %collective-permute-done.5), channel_id=1, source_target_pairs={{0,7},{1,0},{2,1},{3,2},{4,3},{5,4},{6,5},{7,6},{8,15},{9,8},{10,9... | collective-permute-start | bytes 3145736 | tf_op jit(solution)/shard_map/ppermute | solution.py:76
  157.6 3.1 copy-start.3
  159.1 2.0 copy-start.2
  162.6 2.2 copy-start
  175.9 107.6 %all-to-all-start = ((bf16[16,3,4,2,8192]{4,3,2,1,0:T(2,128)(2,1)}), bf16[16,3,4,2,8192]{4,3,2,1,0:T(2,128)(2,1)}, u32[]{:S(2)}, u32[]{:S(2)}) async-start(bf16[16,3,4,2,8192]{4,3,2,1,0:T(2,128)(2,1)} %bitcast.52), calls=%async_computation | async-start | bytes 12582912 | tf_op jit(solution)/shard_map/all_to_all | solution.py:102
  283.5 120.8 %all-to-all-start.1 = ((bf16[16,3,4,2,8192]{4,3,2,1,0:T(2,128)(2,1)}), bf16[16,3,4,2,8192]{4,3,2,1,0:T(2,128)(2,1)}, u32[]{:S(2)}, u32[]{:S(2)}) async-start(bf16[16,3,4,2,8192]{4,3,2,1,0:T(2,128)(2,1)} %bitcast.51), calls=%async_computation.1 | async-start | bytes 12582912 | tf_op jit(solution)/shard_map/all_to_all | solution.py:102
